TPU v7x, 32 devices: a whole 2x2x4 slice. The times are simulated.
32 devices in a mesh: grp: 4 (over z), inner: 8 (over y, x, core).
Axes of the slice: x: 2, y: 2, z: 4, core: 2. Of those that a mesh axis runs over, the one named last changes fastest.
Arguments:
- design: float32 [8, 4096, 1024], P('inner', 'grp'), may hold values from -6 to 6
- row_signs: int32 [8, 4096], P('inner', 'grp'), may hold values from 0 to 1
- kept_rows: int32 [8, 2048], P('inner'), may hold values from 0 to 4095, as said below
Outputs:
- factored: float32 [2048, 1024], P('grp')
Inputs may be any that keep to these rules, and one draw needn't show every extreme that they name: `kept_rows`: within each block the 2048 kept row numbers are distinct, and each block keeps its first and its last row.
All inputs are finite; a program needn't handle non-finite values.
Results may differ from a plain program's by a relative error of at most 0.0048.
Values may be sent and summed in bfloat16 or wider, within the bound.
No kernel may reach another device: no remote copies, remote signals or barrier semaphores. Data moves between devices by JAX's collectives and lax.ppermute only.
A program may use at most 64 MiB of HBM per device.

v0:
```python
import math
import jax
import jax.numpy as jnp
from jax import lax
from jax.sharding import PartitionSpec as P

COLS_DONE = 8
epsilon = 1e-06


def sign_table(row_ids, col_ids):
    common_bits = jnp.bitwise_and(row_ids[:, None], col_ids[None, :])
    ones_total = jnp.zeros(common_bits.shape, jnp.int32)
    for bit_pos in range(4):
        ones_total = ones_total + jnp.bitwise_and(jnp.right_shift(common_bits, bit_pos), 1)
    return 1.0 - 2.0 * jnp.bitwise_and(ones_total, 1).astype(jnp.float32)


def pick_rows(table_rows, chosen_rows):
    return jnp.take(table_rows, chosen_rows, axis=0)


def on_device(design, row_signs, kept_rows):
    block_count, local_rows, columns = design.shape
    keep_count = kept_rows.shape[1]
    groups = lax.axis_size("grp")
    owned_rows = keep_count // groups
    highest = lax.Precision.HIGHEST
    sixteen = jnp.arange(16, dtype=jnp.int32)
    hadamard = sign_table(sixteen, sixteen).astype(jnp.bfloat16)
    flipped = (design * (1 - 2 * row_signs).astype(jnp.float32)[:, :, None]).astype(jnp.bfloat16)
    lowest = flipped.reshape(block_count * local_rows // 16, 16, columns)
    first_pass = jnp.einsum(
        "hc,ncd->nhd", hadamard, lowest, preferred_element_type=jnp.float32
    ).astype(jnp.bfloat16)
    middle_view = first_pass.reshape(block_count * local_rows // 256, 16, 16, columns)
    second_pass = jnp.einsum(
        "hb,mbcd->mhcd", hadamard, middle_view, preferred_element_type=jnp.float32
    ).astype(jnp.bfloat16)
    second_pass = second_pass.reshape(block_count, local_rows, columns)
    gathered_rows = lax.all_to_all(second_pass, "grp", split_axis=2, concat_axis=1, tiled=True)
    col_count = gathered_rows.shape[2]
    by_piece = gathered_rows.reshape(block_count, 16, 256, col_count)
    mixed_rows = jnp.einsum("ha,nakd->nhkd", hadamard, by_piece, preferred_element_type=jnp.float32)
    mixed_rows = mixed_rows.reshape(block_count, 16 * 256, col_count)
    picked = jax.vmap(pick_rows)(mixed_rows, kept_rows)
    partial_value = jnp.sum(picked, axis=0)
    summed = lax.psum(partial_value, "inner")
    sketch = lax.all_to_all(summed, "grp", split_axis=0, concat_axis=1, tiled=True)
    sketch = sketch * (1.0 / (64.0 * math.sqrt(keep_count)))
    row_base = lax.axis_index("grp") * owned_rows
    global_rows = row_base + jnp.arange(owned_rows, dtype=jnp.int32)

    def reflect(col_index, current):
        column = jnp.where(global_rows >= col_index, current[:, col_index], 0.0)
        is_pivot = (global_rows == col_index).astype(jnp.float32)
        norm_sq, crossed, pivot_row = lax.psum(
            (
                jnp.sum(column * column),
                jnp.dot(column, current, precision=highest),
                jnp.dot(is_pivot, current, precision=highest),
            ),
            "grp",
        )
        pivot_value = pivot_row[col_index]
        head_value = -jnp.where(pivot_value >= 0, 1.0, -1.0) * jnp.sqrt(norm_sq)
        length = 2.0 * (norm_sq - head_value * pivot_value) + epsilon
        projected_row = crossed - head_value * pivot_row
        vector = column - head_value * is_pivot
        return current - vector[:, None] * (2.0 * projected_row / length)[None, :]

    result = lax.fori_loop(0, COLS_DONE, reflect, sketch)
    return result


def solution(mesh):
    return jax.shard_map(
        on_device,
        mesh=mesh,
        in_specs=(P("inner", "grp", None), P("inner", "grp"), P("inner", None)),
        out_specs=P("grp", None),
        check_vma=False,
    )
```

profile of v0, /device:TPU:0, one launch (start us, length us, event | category | flops | bytes accessed | tf_op | source)
XLA Modules:
  0.0 397.2 jit_solution(10092679646443896874)
XLA Ops:
  7.2 2.5 multiply_convert_fusion
  13.1 7.7 %copy.22 = bf16[1,1024,1024]{1,0,2:T(2,128)(2,1)} copy(bf16[1,1024,1024]{2,1,0:T(8,128)(2,1)S(1)} %bitcast.77) | data formatting | bytes 4194304 | tf_op jit(solution)/shard_map/reshape | solution.py:40
  21.4 12.8 %reduce.2 = bf16[1024,1024]{1,0:T(8,128)(2,1)S(1)} reduce(bf16[1024,1,1024]{2,1,0:T(2,128)(2,1)} %bitcast.75, bf16[]{:T(256)} %broadcast.106), dimensions={1}, to_apply=%bitcast.43.reduce_sub_computation | reduce | bytes 4194306
  34.2 2.8 reshape.93
  36.9 6.5 %all-to-all-start = ((bf16[4,2,131072]{2,1,0:T(2,128)(2,1)}), bf16[4,2,131072]{2,1,0:T(2,128)(2,1)S(1)}, u32[]{:S(2)}, u32[]{:S(2)}) async-start(bf16[4,2,131072]{2,1,0:T(2,128)(2,1)} %reshape.93), calls=%async_computation | async-start | bytes 4194304 | tf_op jit(solution)/shard_map/all_to_all | solution.py:41
  43.5 48.1 %all-to-all-done = bf16[4,2,131072]{2,1,0:T(2,128)(2,1)S(1)} async-done(((bf16[4,2,131072]{2,1,0:T(2,128)(2,1)}), bf16[4,2,131072]{2,1,0:T(2,128)(2,1)S(1)}, u32[]{:S(2)}, u32[]{:S(2)}) %all-to-all-start) | async-done | bytes 2097184 | tf_op jit(solution)/shard_map/all_to_all | solution.py:41
  91.6 3.4 reshape.94
  94.9 3.0 copy.29
  97.9 2.6 copy.23
  100.5 2.9 convolution_bitcast_fusion
  103.4 4.4 %copy.25 = f32[1,16,256,256]{3,2,1,0:T(8,128)} copy(f32[1,16,256,256]{3,1,2,0:T(8,128)S(1)} %convolution_bitcast_fusion) | data formatting | bytes 8388608 | tf_op jit(solution)/shard_map/ha,nakd->nhkd/transpose | solution.py:44
  107.8 21.4 %gather_fusion = f32[2048,256]{1,0:T(8,128)S(1)} fusion(f32[1,4096,256]{2,1,0:T(8,128)} %bitcast.74, s32[2048]{0:T(1024)S(1)} %bitcast.73), kind=kCustom, calls=%fused_computation | custom fusion | bytes 4210688 | tf_op jit(solution)/shard_map/vmap(jit(_take))/gather | solution.py:20
  130.8 61.1 %all-reduce.5.cloned.1.call-done = f32[4,512,256]{2,1,0:T(8,128)} async-done(((f32[4,512,256]{2,1,0:T(8,128)}), f32[4,512,256]{2,1,0:T(8,128)}) %all-reduce.5.cloned.1.call-update) | async-done | bytes 2097168 | tf_op jit(solution)/shard_map/psum | solution.py:48
  191.9 4.5 %all-to-all-start.1 = ((f32[4,512,256]{2,1,0:T(8,128)}), f32[4,512,256]{2,1,0:T(8,128)S(1)}, u32[]{:S(2)}, u32[]{:S(2)}) async-start(f32[4,512,256]{2,1,0:T(8,128)} %all-reduce.5.cloned.1.call-done), calls=%async_computation.1 | async-start | bytes 4194304 | tf_op jit(solution)/shard_map/all_to_all | solution.py:49
  196.4 47.1 %all-to-all-done.1 = f32[4,512,256]{2,1,0:T(8,128)S(1)} async-done(((f32[4,512,256]{2,1,0:T(8,128)}), f32[4,512,256]{2,1,0:T(8,128)S(1)}, u32[]{:S(2)}, u32[]{:S(2)}) %all-to-all-start.1) | async-done | bytes 2097184 | tf_op jit(solution)/shard_map/all_to_all | solution.py:49
  245.1 1.9 copy.26
  247.0 141.5 %while.14 = (s32[]{:T(128)}, f32[512,1024]{0,1:T(8,128)S(1)}, s32[]{:T(128)}, s32[]{:T(128)}, f32[]{:T(128)}, /*index=5*/f32[]{:T(128)}, f32[]{:T(128)}, f32[]{:T(128)}, f32[]{:T(128)}) while((s32[]{:T(128)}, f32[512,1024]{0,1:T(8,128)S(1)}, s32[]{:T(128)}, s32[]{:T(128)}, f32[]{:T(128)}, /*index=5*/f32[]{:T(128)}, f32[]{:T(128)}, ...), condition=%wide.region_6.7_spmd.clone, body=%wide.region_1.6_spmd.clone.sunk | while | flops 13643786 | bytes 8453379 | solution.py:72
  247.6 1.8 fusion.55
  250.5 10.8 %all-reduce.2 = (f32[1024]{0:T(1024)S(1)}, f32[1024]{0:T(1024)S(1)}, f32[]{:T(128)}) all-reduce(f32[1024]{0:T(1024)S(1)} %bitcast.83, f32[1024]{0:T(1024)S(1)} %bitcast.84, f32[]{:T(128)} %get-tuple-element.117), channel_id=1, replica_groups=mesh['grp'=4,'inner'=8] {'grp'}, use_global_device_ids=true, to_apply=%region_5.5 | all-reduce | flops 2049 | bytes 16392 | tf_op jit(solution)/shard_map/while/body/eval_jaxpr/psum | solution.py:57
  268.7 9.9 %all-reduce.2 = (f32[1024]{0:T(1024)S(1)}, f32[1024]{0:T(1024)S(1)}, f32[]{:T(128)}) all-reduce(f32[1024]{0:T(1024)S(1)} %bitcast.83, f32[1024]{0:T(1024)S(1)} %bitcast.84, f32[]{:T(128)} %get-tuple-element.117), channel_id=1, replica_groups=mesh['grp'=4,'inner'=8] {'grp'}, use_global_device_ids=true, to_apply=%region_5.5 | all-reduce | flops 2049 | bytes 16392 | tf_op jit(solution)/shard_map/while/body/eval_jaxpr/psum | solution.py:57
  285.9 10.8 %all-reduce.2 = (f32[1024]{0:T(1024)S(1)}, f32[1024]{0:T(1024)S(1)}, f32[]{:T(128)}) all-reduce(f32[1024]{0:T(1024)S(1)} %bitcast.83, f32[1024]{0:T(1024)S(1)} %bitcast.84, f32[]{:T(128)} %get-tuple-element.117), channel_id=1, replica_groups=mesh['grp'=4,'inner'=8] {'grp'}, use_global_device_ids=true, to_apply=%region_5.5 | all-reduce | flops 2049 | bytes 16392 | tf_op jit(solution)/shard_map/while/body/eval_jaxpr/psum | solution.py:57
  301.1 1.8 fusion.55
  304.0 9.9 %all-reduce.2 = (f32[1024]{0:T(1024)S(1)}, f32[1024]{0:T(1024)S(1)}, f32[]{:T(128)}) all-reduce(f32[1024]{0:T(1024)S(1)} %bitcast.83, f32[1024]{0:T(1024)S(1)} %bitcast.84, f32[]{:T(128)} %get-tuple-element.117), channel_id=1, replica_groups=mesh['grp'=4,'inner'=8] {'grp'}, use_global_device_ids=true, to_apply=%region_5.5 | all-reduce | flops 2049 | bytes 16392 | tf_op jit(solution)/shard_map/while/body/eval_jaxpr/psum | solution.py:57
  318.4 1.8 fusion.55
  321.3 10.8 %all-reduce.2 = (f32[1024]{0:T(1024)S(1)}, f32[1024]{0:T(1024)S(1)}, f32[]{:T(128)}) all-reduce(f32[1024]{0:T(1024)S(1)} %bitcast.83, f32[1024]{0:T(1024)S(1)} %bitcast.84, f32[]{:T(128)} %get-tuple-element.117), channel_id=1, replica_groups=mesh['grp'=4,'inner'=8] {'grp'}, use_global_device_ids=true, to_apply=%region_5.5 | all-reduce | flops 2049 | bytes 16392 | tf_op jit(solution)/shard_map/while/body/eval_jaxpr/psum | solution.py:57
  336.5 1.8 fusion.55
  339.4 9.9 %all-reduce.2 = (f32[1024]{0:T(1024)S(1)}, f32[1024]{0:T(1024)S(1)}, f32[]{:T(128)}) all-reduce(f32[1024]{0:T(1024)S(1)} %bitcast.83, f32[1024]{0:T(1024)S(1)} %bitcast.84, f32[]{:T(128)} %get-tuple-element.117), channel_id=1, replica_groups=mesh['grp'=4,'inner'=8] {'grp'}, use_global_device_ids=true, to_apply=%region_5.5 | all-reduce | flops 2049 | bytes 16392 | tf_op jit(solution)/shard_map/while/body/eval_jaxpr/psum | solution.py:57
  353.8 1.8 fusion.55
  356.7 10.8 %all-reduce.2 = (f32[1024]{0:T(1024)S(1)}, f32[1024]{0:T(1024)S(1)}, f32[]{:T(128)}) all-reduce(f32[1024]{0:T(1024)S(1)} %bitcast.83, f32[1024]{0:T(1024)S(1)} %bitcast.84, f32[]{:T(128)} %get-tuple-element.117), channel_id=1, replica_groups=mesh['grp'=4,'inner'=8] {'grp'}, use_global_device_ids=true, to_apply=%region_5.5 | all-reduce | flops 2049 | bytes 16392 | tf_op jit(solution)/shard_map/while/body/eval_jaxpr/psum | solution.py:57
  371.9 1.8 fusion.55
  374.8 9.9 %all-reduce.2 = (f32[1024]{0:T(1024)S(1)}, f32[1024]{0:T(1024)S(1)}, f32[]{:T(128)}) all-reduce(f32[1024]{0:T(1024)S(1)} %bitcast.83, f32[1024]{0:T(1024)S(1)} %bitcast.84, f32[]{:T(128)} %get-tuple-element.117), channel_id=1, replica_groups=mesh['grp'=4,'inner'=8] {'grp'}, use_global_device_ids=true, to_apply=%region_5.5 | all-reduce | flops 2049 | bytes 16392 | tf_op jit(solution)/shard_map/while/body/eval_jaxpr/psum | solution.py:57
  388.5 1.8 copy.27
  (97 shorter events, 33.5 us)
Async XLA Ops:
  36.9 6.5 %copy-start = (s32[1,2048]{1,0:T(1,128)S(1)}, s32[1,2048]{1,0:T(1,128)}, u32[]{:S(2)}) copy-start(s32[1,2048]{1,0:T(1,128)} %param.7) | copy-start | bytes 24580
  36.9 54.7 %all-to-all-start = ((bf16[4,2,131072]{2,1,0:T(2,128)(2,1)}), bf16[4,2,131072]{2,1,0:T(2,128)(2,1)S(1)}, u32[]{:S(2)}, u32[]{:S(2)}) async-start(bf16[4,2,131072]{2,1,0:T(2,128)(2,1)} %reshape.93), calls=%async_computation | async-start | bytes 4194304 | tf_op jit(solution)/shard_map/all_to_all | solution.py:41
  43.4 148.5 %all-reduce.5.cloned.1.call-start = ((), (), s32[]{:S(2)}) async-start(), calls=%async_computation.2 | async-start | bytes 4194304 | tf_op jit(solution)/shard_map/psum | solution.py:48
  191.9 51.6 %all-to-all-start.1 = ((f32[4,512,256]{2,1,0:T(8,128)}), f32[4,512,256]{2,1,0:T(8,128)S(1)}, u32[]{:S(2)}, u32[]{:S(2)}) async-start(f32[4,512,256]{2,1,0:T(8,128)} %all-reduce.5.cloned.1.call-done), calls=%async_computation.1 | async-start | bytes 4194304 | tf_op jit(solution)/shard_map/all_to_all | solution.py:49
Sparse Core Ops, SparseCore 0:
  131.0 60.9 all-reduce.4
where the time goes:
time: 398 us; the launch traced here: 397 us
  waiting for transfers between devices  156 us (39%)
  blocking collectives  82.7 us (21%)
  local copies, waits for them, and re-layouts  56 us (14%)
  matrix products  28 us (7%)
  other arithmetic  27.4 us (7%)
  loops' own time  22.4 us (6%)
  between operations  13.5 us (3%)
  starting transfers between devices  11 us (3%)
    psum x8, blocking collectives, reflect(): lax.psum((jnp.sum(column * column), jnp.dot(column, current, precision=hi...  82.7 us
    psum x1, waiting for transfers between devices, on_device(): summed = lax.psum(partial_value, 'inner')  61.1 us
    all_to_all x1, waiting for transfers between devices, on_device(): lax.all_to_all(second_pass, 'grp', split_axis=2, concat_axis=1, tiled=True)  48.1 us
    all_to_all x1, waiting for transfers between devices, on_device(): lax.all_to_all(summed, 'grp', split_axis=0, concat_axis=1, tiled=True)  47.1 us
    another operation x1, loops' own time, on_device(): result = lax.fori_loop(0, COLS_DONE, reflect, sketch)  22.4 us
    gather x2, local copies, waits for them, and re-layouts, pick_rows(): return jnp.take(table_rows, chosen_rows, axis=0)  21.4 us
    dot_general x8, matrix products, reflect(): jnp.dot(column, current, precision=highest)  14.5 us
    unnamed x1, other arithmetic  12.8 us
  transfers between devices with their start and end apart: 3, of which 3 were waited for; matrix products, arithmetic and copies ran while one was open for 0% of the time, Pallas kernels for 0%

commit v1 on v0

--- a/solution.py
+++ b/solution.py
@@ -45,7 +45,7 @@
     mixed_rows = mixed_rows.reshape(block_count, 16 * 256, col_count)
     picked = jax.vmap(pick_rows)(mixed_rows, kept_rows)
     partial_value = jnp.sum(picked, axis=0)
-    summed = lax.psum(partial_value, "inner")
+    summed = jnp.sum(lax.all_gather(partial_value, "inner"), axis=0)
     sketch = lax.all_to_all(summed, "grp", split_axis=0, concat_axis=1, tiled=True)
     sketch = sketch * (1.0 / (64.0 * math.sqrt(keep_count)))
     row_base = lax.axis_index("grp") * owned_rows

time: 398 us -> 435 us (1.093)
  waiting for transfers between devices: 156 us -> 186 us
  other arithmetic: 27.4 us -> 35.9 us
    all_gather x0 -> x1, waiting for transfers between devices: none -> 89 us  [on_device(): summed = jnp.sum(lax.all_gather(partial_value, 'inner'), axis=0)]
    psum x1 -> x0, waiting for transfers between devices: 61.1 us -> none  [on_device(): summed = lax.psum(partial_value, 'inner')]
    reduce_sum x0 -> x1, other arithmetic: none -> 8.45 us  [on_device(): summed = jnp.sum(lax.all_gather(partial_value, 'inner'), axis=0)]
where the time goes in v1:
time: 435 us; the launch traced here: 434 us
  waiting for transfers between devices  186 us (43%)
  blocking collectives  82.7 us (19%)
  local copies, waits for them, and re-layouts  55.6 us (13%)
  other arithmetic  35.9 us (8%)
  matrix products  28 us (6%)
  loops' own time  21.5 us (5%)
  between operations  13.5 us (3%)
  starting transfers between devices  11.1 us (3%)
    all_gather x1, waiting for transfers between devices, on_device(): summed = jnp.sum(lax.all_gather(partial_value, 'inner'), axis=0)  89 us
    psum x8, blocking collectives, reflect(): lax.psum((jnp.sum(column * column), jnp.dot(column, current, precision=hi...  82.7 us
    all_to_all x1, waiting for transfers between devices, on_device(): lax.all_to_all(summed, 'grp', split_axis=0, concat_axis=1, tiled=True)  48.6 us
    all_to_all x1, waiting for transfers between devices, on_device(): lax.all_to_all(second_pass, 'grp', split_axis=2, concat_axis=1, tiled=True)  48.1 us
    another operation x1, loops' own time, on_device(): result = lax.fori_loop(0, COLS_DONE, reflect, sketch)  21.5 us
    gather x2, local copies, waits for them, and re-layouts, pick_rows(): return jnp.take(table_rows, chosen_rows, axis=0)  21.4 us
    dot_general x8, matrix products, reflect(): jnp.dot(column, current, precision=highest)  14.5 us
    unnamed x1, other arithmetic  12.8 us
  transfers between devices with their start and end apart: 3, of which 3 were waited for; matrix products, arithmetic and copies ran while one was open for 0% of the time, Pallas kernels for 0%

profile of v1, /device:TPU:0, one launch (start us, length us, event | category | flops | bytes accessed | tf_op | source)
XLA Modules:
  0.0 433.9 jit_solution(13699200696126563588)
XLA Ops:
  7.2 2.5 multiply_convert_fusion
  13.1 7.7 %copy.27 = bf16[1,1024,1024]{1,0,2:T(2,128)(2,1)} copy(bf16[1,1024,1024]{2,1,0:T(8,128)(2,1)S(1)} %bitcast.79) | data formatting | bytes 4194304 | tf_op jit(solution)/shard_map/reshape | solution.py:40
  21.4 12.8 %reduce.2 = bf16[1024,1024]{1,0:T(8,128)(2,1)S(1)} reduce(bf16[1024,1,1024]{2,1,0:T(2,128)(2,1)} %bitcast.77, bf16[]{:T(256)} %broadcast.129), dimensions={1}, to_apply=%bitcast.45.reduce_sub_computation | reduce | bytes 4194306
  34.2 2.8 reshape.118
  36.9 6.5 %all-to-all-start = ((bf16[4,2,131072]{2,1,0:T(2,128)(2,1)}), bf16[4,2,131072]{2,1,0:T(2,128)(2,1)S(1)}, u32[]{:S(2)}, u32[]{:S(2)}) async-start(bf16[4,2,131072]{2,1,0:T(2,128)(2,1)} %reshape.118), calls=%async_computation | async-start | bytes 4194304 | tf_op jit(solution)/shard_map/all_to_all | solution.py:41
  43.5 48.1 %all-to-all-done = bf16[4,2,131072]{2,1,0:T(2,128)(2,1)S(1)} async-done(((bf16[4,2,131072]{2,1,0:T(2,128)(2,1)}), bf16[4,2,131072]{2,1,0:T(2,128)(2,1)S(1)}, u32[]{:S(2)}, u32[]{:S(2)}) %all-to-all-start) | async-done | bytes 2097184 | tf_op jit(solution)/shard_map/all_to_all | solution.py:41
  91.6 3.4 reshape.119
  94.9 3.0 copy.34
  97.9 2.6 copy.28
  100.5 2.9 convolution_bitcast_fusion
  103.4 4.4 %copy.30 = f32[1,16,256,256]{3,2,1,0:T(8,128)} copy(f32[1,16,256,256]{3,1,2,0:T(8,128)S(1)} %convolution_bitcast_fusion) | data formatting | bytes 8388608 | tf_op jit(solution)/shard_map/ha,nakd->nhkd/transpose | solution.py:44
  107.8 21.4 %gather_fusion = f32[2048,256]{1,0:T(8,128)S(1)} fusion(f32[1,4096,256]{2,1,0:T(8,128)} %bitcast.76, s32[2048]{0:T(1024)S(1)} %bitcast.75), kind=kCustom, calls=%fused_computation | custom fusion | bytes 4210688 | tf_op jit(solution)/shard_map/vmap(jit(_take))/gather | solution.py:20
  130.8 89.0 %all-gather.2.cloned.1.call-done = f32[8,2048,256]{2,1,0:T(8,128)} async-done(((f32[1,2048,256]{2,1,0:T(8,128)}), f32[8,2048,256]{2,1,0:T(8,128)}) %all-gather.2.cloned.1.call-update) | async-done | bytes 16777232 | tf_op jit(solution)/shard_map/all_gather | solution.py:48
  219.9 8.5 %reduce_sum.26 = f32[2048,256]{1,0:T(8,128)} reduce(f32[8,2048,256]{2,1,0:T(8,128)} %all-gather.2.cloned.1.call-done, f32[]{:T(128)} %constant.93.clone.1), dimensions={0}, to_apply=%region_0.1 | reduce | flops 3670016 | bytes 18874372 | tf_op jit(solution)/shard_map/reduce_sum | solution.py:48
  228.3 4.6 %all-to-all-start.1 = ((f32[4,512,256]{2,1,0:T(8,128)}), f32[4,512,256]{2,1,0:T(8,128)S(1)}, u32[]{:S(2)}, u32[]{:S(2)}) async-start(f32[4,512,256]{2,1,0:T(8,128)} %bitcast.84), calls=%async_computation.1 | async-start | bytes 4194304 | tf_op jit(solution)/shard_map/all_to_all | solution.py:49
  232.9 48.6 %all-to-all-done.1 = f32[4,512,256]{2,1,0:T(8,128)S(1)} async-done(((f32[4,512,256]{2,1,0:T(8,128)}), f32[4,512,256]{2,1,0:T(8,128)S(1)}, u32[]{:S(2)}, u32[]{:S(2)}) %all-to-all-start.1) | async-done | bytes 2097184 | tf_op jit(solution)/shard_map/all_to_all | solution.py:49
  283.1 1.9 copy.31
  285.0 140.2 %while.14 = (s32[]{:T(128)}, f32[512,1024]{0,1:T(8,128)S(1)}, s32[]{:T(128)}, s32[]{:T(128)}, f32[]{:T(128)}, /*index=5*/f32[]{:T(128)}, f32[]{:T(128)}, f32[]{:T(128)}, f32[]{:T(128)}) while((s32[]{:T(128)}, f32[512,1024]{0,1:T(8,128)S(1)}, s32[]{:T(128)}, s32[]{:T(128)}, f32[]{:T(128)}, /*index=5*/f32[]{:T(128)}, f32[]{:T(128)}, ...), condition=%wide.region_6.7_spmd.clone, body=%wide.region_1.6_spmd.clone.sunk | while | flops 13643786 | bytes 8453379 | solution.py:72
  288.5 10.8 %all-reduce.2 = (f32[1024]{0:T(1024)S(1)}, f32[1024]{0:T(1024)S(1)}, f32[]{:T(128)}) all-reduce(f32[1024]{0:T(1024)S(1)} %bitcast.85, f32[1024]{0:T(1024)S(1)} %bitcast.86, f32[]{:T(128)} %get-tuple-element.117), channel_id=1, replica_groups=mesh['grp'=4,'inner'=8] {'grp'}, use_global_device_ids=true, to_apply=%region_5.5 | all-reduce | flops 2049 | bytes 16392 | tf_op jit(solution)/shard_map/while/body/eval_jaxpr/psum | solution.py:57
  303.6 1.8 fusion.55
  306.5 9.9 %all-reduce.2 = (f32[1024]{0:T(1024)S(1)}, f32[1024]{0:T(1024)S(1)}, f32[]{:T(128)}) all-reduce(f32[1024]{0:T(1024)S(1)} %bitcast.85, f32[1024]{0:T(1024)S(1)} %bitcast.86, f32[]{:T(128)} %get-tuple-element.117), channel_id=1, replica_groups=mesh['grp'=4,'inner'=8] {'grp'}, use_global_device_ids=true, to_apply=%region_5.5 | all-reduce | flops 2049 | bytes 16392 | tf_op jit(solution)/shard_map/while/body/eval_jaxpr/psum | solution.py:57
  320.7 1.8 fusion.55
  323.6 10.8 %all-reduce.2 = (f32[1024]{0:T(1024)S(1)}, f32[1024]{0:T(1024)S(1)}, f32[]{:T(128)}) all-reduce(f32[1024]{0:T(1024)S(1)} %bitcast.85, f32[1024]{0:T(1024)S(1)} %bitcast.86, f32[]{:T(128)} %get-tuple-element.117), channel_id=1, replica_groups=mesh['grp'=4,'inner'=8] {'grp'}, use_global_device_ids=true, to_apply=%region_5.5 | all-reduce | flops 2049 | bytes 16392 | tf_op jit(solution)/shard_map/while/body/eval_jaxpr/psum | solution.py:57
  341.5 9.9 %all-reduce.2 = (f32[1024]{0:T(1024)S(1)}, f32[1024]{0:T(1024)S(1)}, f32[]{:T(128)}) all-reduce(f32[1024]{0:T(1024)S(1)} %bitcast.85, f32[1024]{0:T(1024)S(1)} %bitcast.86, f32[]{:T(128)} %get-tuple-element.117), channel_id=1, replica_groups=mesh['grp'=4,'inner'=8] {'grp'}, use_global_device_ids=true, to_apply=%region_5.5 | all-reduce | flops 2049 | bytes 16392 | tf_op jit(solution)/shard_map/while/body/eval_jaxpr/psum | solution.py:57
  355.7 1.8 fusion.55
  358.6 10.8 %all-reduce.2 = (f32[1024]{0:T(1024)S(1)}, f32[1024]{0:T(1024)S(1)}, f32[]{:T(128)}) all-reduce(f32[1024]{0:T(1024)S(1)} %bitcast.85, f32[1024]{0:T(1024)S(1)} %bitcast.86, f32[]{:T(128)} %get-tuple-element.117), channel_id=1, replica_groups=mesh['grp'=4,'inner'=8] {'grp'}, use_global_device_ids=true, to_apply=%region_5.5 | all-reduce | flops 2049 | bytes 16392 | tf_op jit(solution)/shard_map/while/body/eval_jaxpr/psum | solution.py:57
  373.7 1.8 fusion.55
  376.6 9.9 %all-reduce.2 = (f32[1024]{0:T(1024)S(1)}, f32[1024]{0:T(1024)S(1)}, f32[]{:T(128)}) all-reduce(f32[1024]{0:T(1024)S(1)} %bitcast.85, f32[1024]{0:T(1024)S(1)} %bitcast.86, f32[]{:T(128)} %get-tuple-element.117), channel_id=1, replica_groups=mesh['grp'=4,'inner'=8] {'grp'}, use_global_device_ids=true, to_apply=%region_5.5 | all-reduce | flops 2049 | bytes 16392 | tf_op jit(solution)/shard_map/while/body/eval_jaxpr/psum | solution.py:57
  393.7 10.8 %all-reduce.2 = (f32[1024]{0:T(1024)S(1)}, f32[1024]{0:T(1024)S(1)}, f32[]{:T(128)}) all-reduce(f32[1024]{0:T(1024)S(1)} %bitcast.85, f32[1024]{0:T(1024)S(1)} %bitcast.86, f32[]{:T(128)} %get-tuple-element.117), channel_id=1, replica_groups=mesh['grp'=4,'inner'=8] {'grp'}, use_global_device_ids=true, to_apply=%region_5.5 | all-reduce | flops 2049 | bytes 16392 | tf_op jit(solution)/shard_map/while/body/eval_jaxpr/psum | solution.py:57
  408.7 1.8 fusion.55
  411.6 9.9 %all-reduce.2 = (f32[1024]{0:T(1024)S(1)}, f32[1024]{0:T(1024)S(1)}, f32[]{:T(128)}) all-reduce(f32[1024]{0:T(1024)S(1)} %bitcast.85, f32[1024]{0:T(1024)S(1)} %bitcast.86, f32[]{:T(128)} %get-tuple-element.117), channel_id=1, replica_groups=mesh['grp'=4,'inner'=8] {'grp'}, use_global_device_ids=true, to_apply=%region_5.5 | all-reduce | flops 2049 | bytes 16392 | tf_op jit(solution)/shard_map/while/body/eval_jaxpr/psum | solution.py:57
  425.2 1.8 copy.32
  (98 shorter events, 34.9 us)
Async XLA Ops:
  36.9 6.5 %copy-start = (s32[1,2048]{1,0:T(1,128)S(1)}, s32[1,2048]{1,0:T(1,128)}, u32[]{:S(2)}) copy-start(s32[1,2048]{1,0:T(1,128)} %param.7) | copy-start | bytes 24580
  36.9 54.7 %all-to-all-start = ((bf16[4,2,131072]{2,1,0:T(2,128)(2,1)}), bf16[4,2,131072]{2,1,0:T(2,128)(2,1)S(1)}, u32[]{:S(2)}, u32[]{:S(2)}) async-start(bf16[4,2,131072]{2,1,0:T(2,128)(2,1)} %reshape.118), calls=%async_computation | async-start | bytes 4194304 | tf_op jit(solution)/shard_map/all_to_all | solution.py:41
  43.4 176.5 %all-gather.2.cloned.1.call-start = ((), (), s32[]{:S(2)}) async-start(), calls=%async_computation.2 | async-start | bytes 18874368 | tf_op jit(solution)/shard_map/all_gather | solution.py:48
  228.3 53.2 %all-to-all-start.1 = ((f32[4,512,256]{2,1,0:T(8,128)}), f32[4,512,256]{2,1,0:T(8,128)S(1)}, u32[]{:S(2)}, u32[]{:S(2)}) async-start(f32[4,512,256]{2,1,0:T(8,128)} %bitcast.84), calls=%async_computation.1 | async-start | bytes 4194304 | tf_op jit(solution)/shard_map/all_to_all | solution.py:49
Sparse Core Ops, SparseCore 0:
  131.0 88.8 all-gather.1
